TPU v7x, 32 devices: a whole 2x2x4 slice. The times are simulated.
32 devices in a mesh: dp: 8 (over z, y), tensor: 4 (over x, core).
Axes of the slice: x: 2, y: 2, z: 4, core: 2. Of those that a mesh axis runs over, the one named last changes fastest.
Arguments:
- tokens: bfloat16 [16384, 1024], P(('dp', 'tensor')), may hold values from -6 to 6
- ln_gain: float32 [1024], replicated, may hold values from 0.1 to 1.9
- ln_bias: float32 [1024], replicated, may hold values from -1.75 to 1.75
- w_qkv: bfloat16 [3, 1024, 16, 64], P(None, None, 'tensor'), may hold values from -0.1875 to 0.1875
- b_qkv: float32 [3, 16, 64], P(None, 'tensor'), may hold values from -3 to 3
- w_in: bfloat16 [1024, 4096], P(None, 'tensor'), may hold values from -0.1875 to 0.1875
- b_in: float32 [4096], P('tensor'), may hold values from -3 to 3
- w_out: bfloat16 [16, 64, 1024], P('tensor'), may hold values from -1.5 to 1.5
- w_down: bfloat16 [4096, 1024], P('tensor'), may hold values from -0.09375 to 0.09375
- b_out: float32 [1024], replicated, may hold values from -3 to 3
- cotangent: bfloat16 [16384, 1024], P(('dp', 'tensor')), may hold values from -6 to 6
- block_doc: int32 [8, 4], P('dp'), may hold values from 0 to 2, as said below
Outputs:
- block_out: bfloat16 [16384, 1024], P(('dp', 'tensor'))
- grad_tokens: float32 [16384, 1024], P(('dp', 'tensor'))
- grad_ln_gain: float32 [1024], replicated
- grad_ln_bias: float32 [1024], replicated
- grad_w_qkv: float32 [3, 1024, 16, 64], P(None, 'dp', 'tensor')
- grad_b_qkv: float32 [3, 16, 64], replicated
- grad_w_in: float32 [1024, 4096], P('dp', 'tensor')
- grad_b_in: float32 [4096], replicated
- grad_w_out: float32 [16, 64, 1024], P('tensor', None, 'dp')
- grad_w_down: float32 [4096, 1024], P('tensor', 'dp')
- grad_b_out: float32 [1024], replicated
Inputs may be any that keep to these rules, and one draw needn't show every extreme that they name: `block_doc`: in each group the numbers start at 0 and rise by 0 or 1 from block to block. Every sequence covers a power of two of blocks, at most 2; a sequence of k blocks starts at a block index divisible by k; each group has a sequence of exactly 2 blocks.
All inputs are finite; a program needn't handle non-finite values.
Results may differ from a plain program's by a relative error of at most 0.012.
The roundings to bfloat16 on the way count: a program that leaves them out, or rounds other values in their place, can miss the bound.
Values may be sent and summed in bfloat16 or wider, within the bound.
No kernel may reach another device: no remote copies, remote signals or barrier semaphores. Data moves between devices by JAX's collectives and lax.ppermute only.
A program may use at most 256 MiB of HBM per device.

v0:
```python
from functools import partial
import jax
import jax.numpy as jnp
from jax import lax
from jax.sharding import PartitionSpec as P

HEADS = 16
FF = 4096
ROT = 16
BLK = 512
epsilon = 1e-05


def layer_norm(rows, ln_gain, ln_bias):
    mean_row = jnp.mean(rows, axis=-1, keepdims=True)
    centred = rows - mean_row
    var_row = jnp.mean(centred * centred, axis=-1, keepdims=True)
    return centred * lax.rsqrt(var_row + epsilon) * ln_gain + ln_bias


def rope_tables(positions):
    half_dims = ROT // 2
    inverse = 1.0 / 10000.0 ** (jnp.arange(half_dims, dtype=jnp.float32) * 2.0 / ROT)
    angles = positions[:, None] * inverse[None, :]
    return (jnp.cos(angles), jnp.sin(angles))


def rotate(vectors, cosine_table, sine_table):
    half_dims = ROT // 2
    leading = vectors[..., :half_dims]
    trailing = vectors[..., half_dims:ROT]
    remain = vectors[..., ROT:]
    cosine = cosine_table[:, None, :]
    sine = sine_table[:, None, :]
    return jnp.concatenate(
        [leading * cosine - trailing * sine, trailing * cosine + leading * sine, remain], axis=-1
    )


def shards(
    tokens, ln_gain, ln_bias, w_qkv, b_qkv, w_in, b_in, w_out, w_down, b_out, cotangent, block_doc
):
    rows_local = tokens.shape[0]
    model_width = tokens.shape[1]
    heads_local = w_qkv.shape[2]
    head_dim = w_qkv.shape[3]
    attn_cols = heads_local * head_dim
    hidden_local = w_in.shape[1]
    score_scale = head_dim ** (-0.5)
    token_values = tokens.astype(jnp.float32)
    normed_rows, ln_back = jax.vjp(layer_norm, token_values, ln_gain, ln_bias)
    normed_low = normed_rows.astype(jnp.bfloat16)
    gathered = lax.all_gather(normed_low, "tensor", axis=0, tiled=True)
    group_rows = gathered.shape[0]
    num_blocks = group_rows // BLK
    seq_blocks = min(4, num_blocks // 2)
    window = seq_blocks * BLK
    pad_rows = window - BLK
    joined_weight = jnp.concatenate(
        [
            w_qkv[0].reshape(model_width, attn_cols),
            w_qkv[1].reshape(model_width, attn_cols),
            w_qkv[2].reshape(model_width, attn_cols),
            w_in,
        ],
        axis=1,
    )
    joined_bias = jnp.concatenate([b_qkv.reshape(3 * attn_cols), b_in])
    upward = jnp.dot(gathered, joined_weight, preferred_element_type=jnp.float32) + joined_bias
    query_pre = upward[:, :attn_cols].reshape(group_rows, heads_local, head_dim)
    key_pre = upward[:, attn_cols : 2 * attn_cols].reshape(group_rows, heads_local, head_dim)
    value_pre = upward[:, 2 * attn_cols : 3 * attn_cols].reshape(group_rows, heads_local, head_dim)
    hidden_pre = upward[:, 3 * attn_cols :]
    sequence_ids = block_doc[0]
    block_starts = jnp.sum(
        (sequence_ids[None, :] < sequence_ids[:, None]).astype(jnp.int32), axis=1
    )
    positions = (
        jnp.arange(group_rows, dtype=jnp.int32) - jnp.repeat(block_starts, BLK) * BLK
    ).astype(jnp.float32)
    cosine_table, sine_table = rope_tables(positions)
    all_queries = rotate(query_pre, cosine_table, sine_table).astype(jnp.bfloat16)
    all_keys = rotate(key_pre, cosine_table, sine_table).astype(jnp.bfloat16)
    all_values = value_pre.astype(jnp.bfloat16)
    pad_heads = jnp.zeros((pad_rows, heads_local, head_dim), jnp.bfloat16)
    keys_padded = jnp.concatenate([pad_heads, all_keys], axis=0)
    values_padded = jnp.concatenate([pad_heads, all_values], axis=0)
    padded_docs = jnp.concatenate([jnp.full((seq_blocks - 1,), -1, jnp.int32), sequence_ids])
    key_docs = jnp.repeat(padded_docs, BLK)
    query_offset = lax.broadcasted_iota(jnp.int32, (BLK, window), 0)
    key_offset = lax.broadcasted_iota(jnp.int32, (BLK, window), 1)
    causal = key_offset - pad_rows <= query_offset

    def window_scores(query_block):
        first_row = query_block * BLK
        query_rows = lax.dynamic_slice_in_dim(all_queries, first_row, BLK, 0)
        key_rows = lax.dynamic_slice_in_dim(keys_padded, first_row, window, 0)
        value_rows = lax.dynamic_slice_in_dim(values_padded, first_row, window, 0)
        window_docs = lax.dynamic_slice_in_dim(key_docs, first_row, window, 0)
        allowed = (window_docs[None, :] == sequence_ids[query_block]) & causal
        scores = (
            jnp.einsum("qhe,khe->hqk", query_rows, key_rows, preferred_element_type=jnp.float32)
            * score_scale
        )
        return (query_rows, key_rows, value_rows, jnp.where(allowed[None], scores, -1e30))

    def attend(query_block):
        query_rows, key_rows, value_rows, scores = window_scores(query_block)
        maxima = jnp.max(scores, axis=-1)
        log_total = maxima + jnp.log(jnp.sum(jnp.exp(scores - maxima[..., None]), axis=-1))
        weights = jax.nn.softmax(scores, axis=-1).astype(jnp.bfloat16)
        out_rows = jnp.einsum(
            "hqk,khe->qhe", weights, value_rows, preferred_element_type=jnp.float32
        )
        return (out_rows, log_total)

    attended_blocks, log_totals = lax.map(attend, jnp.arange(num_blocks, dtype=jnp.int32))
    attended = attended_blocks.reshape(group_rows, attn_cols).astype(jnp.bfloat16)
    w_out_flat = w_out.reshape(attn_cols, model_width)
    active_full, gelu_back = jax.vjp(partial(jax.nn.gelu, approximate=False), hidden_pre)
    active = active_full.astype(jnp.bfloat16)
    active_rows = lax.dynamic_slice_in_dim(
        active, jnp.int32(0), rows_local * lax.axis_size("tensor"), 0
    )
    mixed = lax.psum_scatter(
        jnp.dot(attended, w_out_flat, preferred_element_type=jnp.float32)
        + jnp.dot(active_rows, w_down, preferred_element_type=jnp.float32),
        "tensor",
        scatter_dimension=0,
        tiled=True,
    )
    block_out = (token_values + mixed + b_out).astype(jnp.bfloat16)
    cotangent_group = lax.all_gather(cotangent, "tensor", axis=0, tiled=True)
    grad_attended = jnp.einsum(
        "td,cd->tc", cotangent_group, w_out_flat, preferred_element_type=jnp.float32
    ).astype(jnp.bfloat16)
    grad_active = jnp.einsum(
        "td,fd->tf", cotangent_group, w_down, preferred_element_type=jnp.float32
    )
    grad_w_out = jnp.einsum(
        "tc,td->cd", attended, cotangent_group, preferred_element_type=jnp.float32
    )
    grad_w_down = jnp.einsum(
        "tf,td->fd", active, cotangent_group, preferred_element_type=jnp.float32
    )
    grad_hidden = gelu_back(grad_active)[0].astype(jnp.bfloat16)
    grad_out_heads = grad_attended.reshape(group_rows, heads_local, head_dim)

    def back_block(query_block, carried):
        grad_q_all, grad_k_padded, grad_v_padded = carried
        first_row = query_block * BLK
        query_rows, key_rows, value_rows, scores = window_scores(query_block)
        grad_rows_out = lax.dynamic_slice_in_dim(grad_out_heads, first_row, BLK, 0)
        weights = jnp.exp(scores - log_totals[query_block][..., None])
        grad_weights = jnp.einsum(
            "qhe,khe->hqk", grad_rows_out, value_rows, preferred_element_type=jnp.float32
        )
        deltas = jnp.sum(weights * grad_weights, axis=-1)
        grad_scores = (weights * (grad_weights - deltas[..., None])).astype(jnp.bfloat16)
        grad_q_rows = (
            jnp.einsum("hqk,khe->qhe", grad_scores, key_rows, preferred_element_type=jnp.float32)
            * score_scale
        )
        grad_k_rows = (
            jnp.einsum("hqk,qhe->khe", grad_scores, query_rows, preferred_element_type=jnp.float32)
            * score_scale
        )
        grad_v_rows = jnp.einsum(
            "hqk,qhe->khe",
            weights.astype(jnp.bfloat16),
            grad_rows_out,
            preferred_element_type=jnp.float32,
        )
        old_k = lax.dynamic_slice_in_dim(grad_k_padded, first_row, window, 0)
        old_v = lax.dynamic_slice_in_dim(grad_v_padded, first_row, window, 0)
        grad_k_padded = lax.dynamic_update_slice_in_dim(
            grad_k_padded, old_k + grad_k_rows, first_row, 0
        )
        grad_v_padded = lax.dynamic_update_slice_in_dim(
            grad_v_padded, old_v + grad_v_rows, first_row, 0
        )
        grad_q_all = lax.dynamic_update_slice_in_dim(grad_q_all, grad_q_rows, first_row, 0)
        return (grad_q_all, grad_k_padded, grad_v_padded)

    zero_heads = jnp.zeros((group_rows, heads_local, head_dim), jnp.float32)
    zero_padded = jnp.zeros((group_rows + pad_rows, heads_local, head_dim), jnp.float32)
    grad_queries, grad_k_padded, grad_v_padded = lax.fori_loop(
        0, num_blocks, back_block, (zero_heads, zero_padded, zero_padded)
    )
    grad_keys = grad_k_padded[pad_rows:]
    grad_values = grad_v_padded[pad_rows:]
    grad_q_pre = (
        rotate(grad_queries, cosine_table, -sine_table)
        .astype(jnp.bfloat16)
        .reshape(group_rows, attn_cols)
    )
    grad_k_pre = (
        rotate(grad_keys, cosine_table, -sine_table)
        .astype(jnp.bfloat16)
        .reshape(group_rows, attn_cols)
    )
    grad_v_pre = grad_values.astype(jnp.bfloat16).reshape(group_rows, attn_cols)
    grad_upward = jnp.concatenate([grad_q_pre, grad_k_pre, grad_v_pre, grad_hidden], axis=1)
    grad_joined_weight = jnp.einsum(
        "td,tc->dc", gathered, grad_upward, preferred_element_type=jnp.float32
    )
    grad_joined_bias = jnp.sum(grad_upward, axis=0, dtype=jnp.float32)
    grad_normed = lax.psum_scatter(
        jnp.einsum("tc,dc->td", grad_upward, joined_weight, preferred_element_type=jnp.float32),
        "tensor",
        scatter_dimension=0,
        tiled=True,
    )
    grad_tokens_norm, grad_gain_part, grad_bias_part = ln_back(grad_normed)
    grad_tokens = grad_tokens_norm + cotangent.astype(jnp.float32)
    grad_bout_part = jnp.sum(cotangent, axis=0, dtype=jnp.float32)
    grad_w_qkv_local = jnp.stack(
        [
            grad_joined_weight[:, member * attn_cols : (member + 1) * attn_cols].reshape(
                model_width, heads_local, head_dim
            )
            for member in range(3)
        ]
    )
    grad_w_in_local = grad_joined_weight[:, 3 * attn_cols :]
    tensor_rank = lax.axis_index("tensor")
    bqkv_full = lax.dynamic_update_slice(
        jnp.zeros((3, HEADS, head_dim), jnp.float32),
        grad_joined_bias[: 3 * attn_cols].reshape(3, heads_local, head_dim),
        (jnp.int32(0), tensor_rank * heads_local, jnp.int32(0)),
    )
    bin_full = lax.dynamic_update_slice(
        jnp.zeros((FF,), jnp.float32),
        grad_joined_bias[3 * attn_cols :],
        (tensor_rank * hidden_local,),
    )
    grad_ln_gain, grad_ln_bias, grad_b_out, grad_b_qkv, grad_b_in = lax.psum(
        (grad_gain_part, grad_bias_part, grad_bout_part, bqkv_full, bin_full), ("dp", "tensor")
    )
    grad_w_qkv, grad_w_in, grad_w_out_part, grad_w_down_part = (
        lax.psum_scatter(grad_w_qkv_local, "dp", scatter_dimension=1, tiled=True),
        lax.psum_scatter(grad_w_in_local, "dp", scatter_dimension=0, tiled=True),
        lax.psum_scatter(
            grad_w_out.reshape(heads_local, head_dim, model_width),
            "dp",
            scatter_dimension=2,
            tiled=True,
        ),
        lax.psum_scatter(grad_w_down, "dp", scatter_dimension=1, tiled=True),
    )
    return (
        block_out,
        grad_tokens,
        grad_ln_gain,
        grad_ln_bias,
        grad_w_qkv,
        grad_b_qkv,
        grad_w_in,
        grad_b_in,
        grad_w_out_part,
        grad_w_down_part,
        grad_b_out,
    )


def solution(mesh):
    return jax.shard_map(
        shards,
        mesh=mesh,
        in_specs=(
            P(("dp", "tensor"), None),
            P(),
            P(),
            P(None, None, "tensor", None),
            P(None, "tensor", None),
            P(None, "tensor"),
            P("tensor"),
            P("tensor", None, None),
            P("tensor", None),
            P(),
            P(("dp", "tensor"), None),
            P("dp", None),
        ),
        out_specs=(
            P(("dp", "tensor"), None),
            P(("dp", "tensor"), None),
            P(),
            P(),
            P(None, "dp", "tensor", None),
            P(),
            P("dp", "tensor"),
            P(),
            P("tensor", None, "dp"),
            P("tensor", "dp"),
            P(),
        ),
        check_vma=False,
    )
```

profile of v0, /device:TPU:0, one launch (start us, length us, event | category | flops | bytes accessed | tf_op | source)
XLA Modules:
  0.0 755.2 jit_solution(2105448763767745747)
XLA Ops:
  22.3 29.4 %all-gather.3.cloned.1.call-done = bf16[2048,1024]{1,0:T(8,128)(2,1)} async-done(((bf16[512,1024]{1,0:T(8,128)(2,1)}), bf16[2048,1024]{1,0:T(8,128)(2,1)}) %all-gather.3.cloned.1.call-update) | async-done | bytes 4194320 | tf_op jit(solution)/shard_map/all_gather | solution.py:53
  51.7 14.2 %convolution_add_fusion = f32[2048,1792]{0,1:T(8,128)} fusion(bf16[2048,1024]{1,0:T(8,128)(2,1)} %all-gather.3.cloned.1.call-done, f32[1792]{0:T(1024)S(1)} %pad_maximum_fusion.8, bf16[1024,1024]{1,0:T(8,128)(2,1)} %param.21, bf16[1024,256]{1,0:T(8,128)(2,1)S(1)} %copy.38, bf16[1024,256]{1,0:T(8,128)(2,1)} %copy.37, bf16[1024,256]{1,0:T(8,128)(2,1)} %copy.36), kind=kOutput, calls=%fused_computation.77 | convolution fusion | flops 7534542848 | bytes 22551552 | tf_op jit(solution)/shard_map/dot_general | solution.py:69
  74.0 59.7 %while.31 = (s32[]{:T(128)}, bf16[4,512,4,64]{1,3,2,0:T(8,128)(2,1)}, f32[4,4,512]{2,1,0:T(4,128)}, s32[4]{0:T(128)S(1)}, bf16[2560,4,64]{0,2,1:T(8,128)(2,1)}, ...) while((s32[]{:T(128)}, ...), condition=%wide.region_6.7_spmd.clone, body=%wide.region_3.6_spmd.clone.sunk | while | flops 563084288 | bytes 29175080 | solution.py:117
  133.8 4.7 convolution_convert_fusion
  143.6 80.2 %while.32 = (s32[]{:T(128)}, f32[2048,4,64]{0,2,1:T(8,128)}, f32[2560,4,64]{0,2,1:T(8,128)}, f32[2560,4,64]{0,2,1:T(8,128)}, bf16[2560,4,64]{0,2,1:T(8,128)(2,1)...) while((s32[]{:T(128)}, f32[2048,4,64]{0,2,1:T(8,128)}, ...), condition=%wide.region_10.11_spmd.clone, body=%wide.region_8.10_spmd.clone.sunk | while | flops 1375599616 | bytes 97585616 | solution.py:187
  159.4 4.5 fusion.143
  179.4 4.5 fusion.143
  199.3 4.5 fusion.143
  219.3 4.5 fusion.143
  230.4 26.7 %add_convert_fusion = (bf16[2048,1024]{0,1:T(8,128)(2,1)S(1)}, f32[2048,1024]{0,1:T(8,128)}) fusion(f32[2048,1792]{0,1:T(8,128)} %convolution_add_fusion, bf16[2048,1024]{1,0:T(8,128)(2,1)S(1)} %copy-done.29, bf16[1024,1024]{1,0:T(8,128)(2,1)S(1)} %copy-done), kind=kOutput, calls=%fused_computation.61 | convolution fusion | flops 4445962240 | bytes 27262976 | tf_op jit(solution)/shard_map/td,fd->tf/dot_general | solution.py:137
  259.2 12.7 %fusion.79 = f32[2048,1024]{1,0:T(8,128)} fusion(bf16[1024,1024]{1,0:T(8,128)(2,1)} %param.21, bf16[1024,256]{1,0:T(8,128)(2,1)S(1)} %copy-done.17, bf16[1024,256]{1,0:T(8,128)(2,1)S(1)} %copy-done.15, bf16[1024,256]{1,0:T(8,128)(2,1)S(1)} %copy-done.14, bf16[2048,1024]{0,1:T(8,128)(2,1)S(1)} %get-tuple-element.373, bf16[2048,256]{0,1:T(8,128)(2,1)S(1)} %bitcast.104, ...), kind=kOutput, calls=%fused_computation.119 | convolution fusion | flops 7560232960 | bytes 19398656 | tf_op jit(solution)/shard_map/tc,dc->td/dot_general | solution.py:209
  274.4 11.8 %multiply_convert_fusion.1 = bf16[2048,1024]{0,1:T(8,128)(2,1)} fusion(f32[2048,1024]{0,1:T(8,128)} %get-tuple-element.374, f32[2048,1792]{0,1:T(8,128)} %convolution_add_fusion), kind=kLoop, calls=%fused_computation.62 | loop fusion | flops 6291456 | bytes 20971520 | tf_op jit(solution)/shard_map/convert_element_type | solution.py:121
  286.2 6.6 fusion.91
  292.8 4.8 convolution_add_fusion.1
  302.4 12.4 %fusion.85 = f32[1024,1792]{1,0:T(8,128)S(1)} fusion(bf16[2048,1024]{1,0:T(8,128)(2,1)} %all-gather.3.cloned.1.call-done, bf16[2048,1024]{0,1:T(8,128)(2,1)} %copy-done.6, bf16[2048,256]{0,1:T(8,128)(2,1)} %bitcast.105, bf16[2048,256]{0,1:T(8,128)(2,1)} %bitcast.114, bf16[2048,256]{0,1:T(8,128)(2,1)} %bitcast.111), kind=kOutput, calls=%fused_computation.149 | convolution fusion | flops 7545552896 | bytes 18874368 | tf_op jit(solution)/shard_map/td,tc->dc/dot_general | solution.py:204
  330.0 4.8 slice.139
  335.1 10.1 %fusion.92 = f32[1024,1024]{1,0:T(8,128)} fusion(bf16[2048,1024]{0,1:T(8,128)(2,1)} %multiply_convert_fusion.1, bf16[2048,1024]{1,0:T(8,128)(2,1)} %all-gather.5.cloned.1.call-done), kind=kOutput, calls=%fused_computation.155 | convolution fusion | flops 4294967296 | bytes 12582912 | tf_op jit(solution)/shard_map/tf,td->fd/dot_general | solution.py:143
  354.4 63.1 %reduce-scatter.7.cloned.1.call-done = f32[512,1024]{1,0:T(8,128)} async-done(((f32[2048,1024]{1,0:T(8,128)}), f32[512,1024]{1,0:T(8,128)}) %reduce-scatter.7.cloned.1.call-update) | async-done | bytes 2097168 | tf_op jit(solution)/shard_map/reduce_scatter | solution.py:125
  417.5 5.1 convert_reduce_fusion.2
  422.7 40.9 %all-reduce.2 = (f32[1024]{0:T(1024)}, f32[1024]{0:T(1024)}, f32[3,16,64]{2,1,0:T(8,128)}, f32[4096]{0:T(1024)}, f32[1024]{0:T(1024)}) all-reduce(f32[1024]{0:T(1024)S(1)} %get-tuple-element.320, f32[1024]{0:T(1024)S(1)} %get-tuple-element.322, ...), channel_id=1, replica_groups=mesh['dp'=8,'tensor'=4] {'dp','tensor'}, use_global_device_ids=true, to_apply=%region_15.16 | all-reduce | flops 10240 | bytes 81920 | tf_op jit(solution)/shard_map/psum | solution.py:237
  463.6 22.5 %reduce-scatter.15.cloned.1.call-done = f32[4,64,128]{2,1,0:T(8,128)} async-done(((f32[4,64,1024]{2,1,0:T(8,128)}), f32[4,64,128]{2,1,0:T(8,128)}) %reduce-scatter.15.cloned.1.call-update) | async-done | bytes 131088 | tf_op jit(solution)/shard_map/reduce_scatter | solution.py:243
  486.1 77.8 %reduce-scatter.11.cloned.1.call-done = f32[3,128,4,64]{1,3,2,0:T(8,128)} async-done(((f32[3,1024,4,64]{1,3,2,0:T(8,128)}), f32[3,128,4,64]{1,3,2,0:T(8,128)}) %reduce-scatter.11.cloned.1.call-update) | async-done | bytes 393232 | tf_op jit(solution)/shard_map/reduce_scatter | solution.py:241
  563.8 91.7 %reduce-scatter.13.cloned.1.call-done = f32[128,1024]{1,0:T(8,128)} async-done(((f32[1024,1024]{1,0:T(8,128)}), f32[128,1024]{1,0:T(8,128)}) %reduce-scatter.13.cloned.1.call-update) | async-done | bytes 524304 | tf_op jit(solution)/shard_map/reduce_scatter | solution.py:242
  655.5 92.6 %reduce-scatter.17.cloned.1.call-done = f32[1024,128]{1,0:T(8,128)} async-done(((f32[1024,1024]{1,0:T(8,128)}), f32[1024,128]{1,0:T(8,128)}) %reduce-scatter.17.cloned.1.call-update) | async-done | bytes 524304 | tf_op jit(solution)/shard_map/reduce_scatter | solution.py:249
  (234 shorter events, 179.8 us)
Async XLA Ops:
  7.2 223.1 %copy-start = (bf16[1024,1024]{1,0:T(8,128)(2,1)S(1)}, bf16[1024,1024]{1,0:T(8,128)(2,1)}, u32[]{:S(2)}) copy-start(bf16[1024,1024]{1,0:T(8,128)(2,1)} %param.24) | copy-start | bytes 6291460
  7.2 13.6 %copy-start.26 = (f32[3,4,64]{2,1,0:T(4,128)S(1)}, f32[3,4,64]{2,1,0:T(4,128)}, u32[]{:S(2)}) copy-start(f32[3,4,64]{2,1,0:T(4,128)} %param.20) | copy-start | bytes 9220
  7.2 13.7 %copy-start.30 = (s32[1,4]{1,0:T(1,128)S(1)}, s32[1,4]{1,0:T(1,128)}, u32[]{:S(2)}) copy-start(s32[1,4]{1,0:T(1,128)} %param.27) | copy-start | bytes 52
  7.2 14.1 %copy-start.28 = (f32[1024]{0:T(1024)S(1)}, f32[1024]{0:T(1024)}, u32[]{:S(2)}) copy-start(f32[1024]{0:T(1024)} %param.22) | copy-start | bytes 12292
  7.2 44.5 %all-gather.3.cloned.1.call-start = ((), (), s32[]{:S(2)}) async-start(), calls=%async_computation.6 | async-start | bytes 5242880 | tf_op jit(solution)/shard_map/all_gather | solution.py:53
  14.4 119.4 %all-gather.5.cloned.1.call-start = ((), (), s32[]{:S(2)}) async-start(), calls=%async_computation.8 | async-start | bytes 5242880 | tf_op jit(solution)/shard_map/all_gather | solution.py:133
  15.1 334.6 %reduce-scatter.9.cloned.1.call-start = ((), (), s32[]{:S(2)}) async-start(), calls=%async_computation.9 | async-start | bytes 10485760 | tf_op jit(solution)/shard_map/reduce_scatter | solution.py:208
  20.8 45.1 %copy-start.16 = (bf16[1024,256]{1,0:T(8,128)(2,1)}, bf16[1024,256]{1,0:T(8,128)(2,1)S(1)}, u32[]{:S(2)}) copy-start(bf16[1024,256]{1,0:T(8,128)(2,1)S(1)} %copy.38) | copy-start | bytes 1572868
  22.3 48.1 %copy-start.11 = (f32[2048,8]{0,1:T(8,128)}, f32[2048,8]{0,1:T(8,128)S(1)}, u32[]{:S(2)}) copy-start(f32[2048,8]{0,1:T(8,128)S(1)} %get-tuple-element.404) | copy-start | bytes 196612
  133.8 9.9 %copy-start.1 = (bf16[2560,4,64]{0,2,1:T(8,128)(2,1)S(1)}, bf16[2560,4,64]{0,2,1:T(8,128)(2,1)}, u32[]{:S(2)}) copy-start(bf16[2560,4,64]{0,2,1:T(8,128)(2,1)} %get-tuple-element.658) | copy-start | bytes 3932164
  143.6 83.4 %copy-start.12 = (f32[2048,8]{0,1:T(8,128)S(1)}, f32[2048,8]{0,1:T(8,128)}, u32[]{:S(2)}) copy-start(f32[2048,8]{0,1:T(8,128)} %copy-done.11) | copy-start | bytes 196612
  143.6 83.4 %copy-start.18 = (f32[2048,8]{0,1:T(8,128)S(1)}, f32[2048,8]{0,1:T(8,128)}, u32[]{:S(2)}) copy-start(f32[2048,8]{0,1:T(8,128)} %get-tuple-element.402) | copy-start | bytes 196612
  230.2 27.0 %copy-start.7 = (bf16[2048,4,64]{0,2,1:T(8,128)(2,1)}, bf16[2048,4,64]{0,2,1:T(8,128)(2,1)S(1)}, u32[]{:S(2)}) copy-start(bf16[2048,4,64]{0,2,1:T(8,128)(2,1)S(1)} %slice.174) | copy-start | bytes 3145732
  230.3 26.8 %copy-start.8 = (bf16[2048,4,64]{0,2,1:T(8,128)(2,1)}, bf16[2048,4,64]{0,2,1:T(8,128)(2,1)S(1)}, u32[]{:S(2)}) copy-start(bf16[2048,4,64]{0,2,1:T(8,128)(2,1)S(1)} %get-tuple-element.405) | copy-start | bytes 3145732
  230.4 26.8 %copy-start.9 = (bf16[2048,4,64]{0,2,1:T(8,128)(2,1)}, bf16[2048,4,64]{0,2,1:T(8,128)(2,1)S(1)}, u32[]{:S(2)}) copy-start(bf16[2048,4,64]{0,2,1:T(8,128)(2,1)S(1)} %get-tuple-element.406) | copy-start | bytes 3145732
  230.4 28.8 %copy-start.14 = (bf16[1024,256]{1,0:T(8,128)(2,1)S(1)}, bf16[1024,256]{1,0:T(8,128)(2,1)}, u32[]{:S(2)}) copy-start(bf16[1024,256]{1,0:T(8,128)(2,1)} %copy.36) | copy-start | bytes 1572868
  230.4 28.8 %copy-start.15 = (bf16[1024,256]{1,0:T(8,128)(2,1)S(1)}, bf16[1024,256]{1,0:T(8,128)(2,1)}, u32[]{:S(2)}) copy-start(bf16[1024,256]{1,0:T(8,128)(2,1)} %copy.37) | copy-start | bytes 1572868
  230.4 28.8 %copy-start.17 = (bf16[1024,256]{1,0:T(8,128)(2,1)S(1)}, bf16[1024,256]{1,0:T(8,128)(2,1)}, u32[]{:S(2)}) copy-start(bf16[1024,256]{1,0:T(8,128)(2,1)} %copy-done.16) | copy-start | bytes 1572868
  271.9 145.6 %reduce-scatter.7.cloned.1.call-start = ((), (), s32[]{:S(2)}) async-start(), calls=%async_computation.7 | async-start | bytes 10485760 | tf_op jit(solution)/shard_map/reduce_scatter | solution.py:125
  297.6 188.5 %reduce-scatter.15.cloned.1.call-start = ((), (), s32[]{:S(2)}) async-start(), calls=%async_computation.12 | async-start | bytes 1179648 | tf_op jit(solution)/shard_map/reduce_scatter | solution.py:243
  302.1 261.7 %reduce-scatter.11.cloned.1.call-start = ((), (), s32[]{:S(2)}) async-start(), calls=%async_computation.10 | async-start | bytes 3538944 | tf_op jit(solution)/shard_map/reduce_scatter | solution.py:241
  329.9 325.6 %reduce-scatter.13.cloned.1.call-start = ((), (), s32[]{:S(2)}) async-start(), calls=%async_computation.11 | async-start | bytes 4718592 | tf_op jit(solution)/shard_map/reduce_scatter | solution.py:242
  334.8 413.3 %reduce-scatter.17.cloned.1.call-start = ((), (), s32[]{:S(2)}) async-start(), calls=%async_computation.13 | async-start | bytes 4718592 | tf_op jit(solution)/shard_map/reduce_scatter | solution.py:249
  345.2 72.3 %copy-start.27 = (f32[1024]{0:T(1024)S(1)}, f32[1024]{0:T(1024)}, u32[]{:S(2)}) copy-start(f32[1024]{0:T(1024)} %param.25) | copy-start | bytes 12292
  (28 other events, 95.1 us)
Sparse Core Ops, SparseCore 0:
  14.5 37.1 all-gather.2
  53.3 34.5 all-gather.4
  272.0 71.5 reduce-scatter.8
  346.1 71.4 reduce-scatter.6
  421.3 64.6 reduce-scatter.14
  490.1 73.6 reduce-scatter.10
  568.0 87.4 reduce-scatter.12
  659.7 88.3 reduce-scatter.16
where the time goes:
time: 760 us; the launch traced here: 755 us
  waiting for transfers between devices  378 us (50%)
  matrix products  185 us (24%)
  other arithmetic  70.6 us (9%)
  local copies, waits for them, and re-layouts  53.6 us (7%)
  blocking collectives  40.9 us (5%)
  between operations  14.9 us (2%)
  loops' own time  10.9 us (1%)
    reduce_scatter x1, waiting for transfers between devices, shards(): lax.psum_scatter(grad_w_down, 'dp', scatter_dimension=1, tiled=True)  92.6 us
    reduce_scatter x1, waiting for transfers between devices, shards(): lax.psum_scatter(grad_w_in_local, 'dp', scatter_dimension=0, tiled=True)  91.7 us
    reduce_scatter x1, waiting for transfers between devices, shards(): lax.psum_scatter(grad_w_qkv_local, 'dp', scatter_dimension=1, tiled=True)  77.8 us
    reduce_scatter x1, waiting for transfers between devices, shards(): lax.psum_scatter(jnp.dot(attended, w_out_flat, preferred_element_type=jnp...  63.1 us
    psum x1, blocking collectives, shards(): lax.psum((grad_gain_part, grad_bias_part, grad_bout_part, bqkv_full, bin_...  40.9 us
    all_gather x1, waiting for transfers between devices, shards(): gathered = lax.all_gather(normed_low, 'tensor', axis=0, tiled=True)  29.4 us
    dot_general x1, matrix products, shards(): jnp.einsum('td,fd->tf', cotangent_group, w_down, preferred_element_type=j...  26.7 us
    reduce_scatter x1, waiting for transfers between devices, shards(): lax.psum_scatter(grad_w_out.reshape(heads_local, head_dim, model_width),...  22.5 us
  transfers between devices with their start and end apart: 8, of which 6 were waited for; matrix products, arithmetic and copies ran while one was open for 21% of the time, Pallas kernels for 0%

commit v1 on v0

--- a/solution.py
+++ b/solution.py
@@ -50,7 +50,19 @@
     token_values = tokens.astype(jnp.float32)
     normed_rows, ln_back = jax.vjp(layer_norm, token_values, ln_gain, ln_bias)
     normed_low = normed_rows.astype(jnp.bfloat16)
-    gathered = lax.all_gather(normed_low, "tensor", axis=0, tiled=True)
+    mid_arr = lax.axis_size("tensor")
+    everything = lax.axis_index("tensor")
+    block_now, mat_out, met_up = (mid_arr, everything, normed_low.shape[0])
+    oldest, side_arr = (normed_low, 1)
+    while side_arr < block_now:
+        step_out = lax.ppermute(
+            oldest,
+            axis_name="tensor",
+            perm=[(nth, (nth - side_arr) % block_now) for nth in range(block_now)],
+        )
+        oldest = jnp.concatenate([oldest, step_out], axis=0)
+        side_arr = 2 * side_arr
+    gathered = jnp.roll(oldest, mat_out * met_up, axis=0)
     group_rows = gathered.shape[0]
     num_blocks = group_rows // BLK
     seq_blocks = min(4, num_blocks // 2)

time: 760 us -> 816 us (1.074)
  waiting for transfers between devices: 378 us -> 414 us
  local copies, waits for them, and re-layouts: 53.6 us -> 68.1 us
    ppermute x0 -> x2, waiting for transfers between devices: none -> 65.3 us  [shards(): lax.ppermute(oldest, axis_name='tensor', perm=[(nth, (nth - side_arr) % b...]
    all_gather x1 -> x0, waiting for transfers between devices: 29.4 us -> none  [shards(): gathered = lax.all_gather(normed_low, 'tensor', axis=0, tiled=True)]
    unnamed x59 -> x69, local copies, waits for them, and re-layouts: 6.61 us -> 15.1 us
  transfers between devices with their start and end apart: 8 -> 9, of which waited for: 6 -> 7; matrix products, arithmetic and copies ran while one was open for 21% -> 22% of each run, Pallas kernels for 0% -> 0%
where the time goes in v1:
time: 816 us; the launch traced here: 811 us
  waiting for transfers between devices  414 us (51%)
  matrix products  185 us (23%)
  other arithmetic  73.5 us (9%)
  local copies, waits for them, and re-layouts  68.1 us (8%)
  blocking collectives  40.9 us (5%)
  between operations  14.9 us (2%)
  loops' own time  10.9 us (1%)
    reduce_scatter x1, waiting for transfers between devices, shards(): lax.psum_scatter(grad_w_down, 'dp', scatter_dimension=1, tiled=True)  92.5 us
    reduce_scatter x1, waiting for transfers between devices, shards(): lax.psum_scatter(grad_w_in_local, 'dp', scatter_dimension=0, tiled=True)  91.5 us
    reduce_scatter x1, waiting for transfers between devices, shards(): lax.psum_scatter(grad_w_qkv_local, 'dp', scatter_dimension=1, tiled=True)  78.1 us
    ppermute x2, waiting for transfers between devices, shards(): lax.ppermute(oldest, axis_name='tensor', perm=[(nth, (nth - side_arr) % b...  65.3 us
    reduce_scatter x1, waiting for transfers between devices, shards(): lax.psum_scatter(jnp.dot(attended, w_out_flat, preferred_element_type=jnp...  63.7 us
    psum x1, blocking collectives, shards(): lax.psum((grad_gain_part, grad_bias_part, grad_bout_part, bqkv_full, bin_...  40.9 us
    dot_general x1, matrix products, shards(): jnp.einsum('td,fd->tf', cotangent_group, w_down, preferred_element_type=j...  26.7 us
    reduce_scatter x1, waiting for transfers between devices, shards(): lax.psum_scatter(grad_w_out.reshape(heads_local, head_dim, model_width),...  22.8 us
  transfers between devices with their start and end apart: 9, of which 7 were waited for; matrix products, arithmetic and copies ran while one was open for 22% of the time, Pallas kernels for 0%

profile of v1, /device:TPU:0, one launch (start us, length us, event | category | flops | bytes accessed | tf_op | source)
XLA Modules:
  0.0 811.0 jit_solution(9306469256474887805)
XLA Ops:
  16.3 19.0 %collective-permute-done = bf16[512,1024]{1,0:T(8,128)(2,1)} collective-permute-done((bf16[512,1024]{1,0:T(8,128)(2,1)S(1)}, bf16[512,1024]{1,0:T(8,128)(2,1)}, u32[]{:S(2)}, u32[]{:S(2)}) %collective-permute-start) | collective-permute-done | bytes 1048608 | tf_op jit(solution)/shard_map/ppermute | solution.py:58
  50.8 46.3 %collective-permute-done.1 = bf16[1024,1024]{1,0:T(8,128)(2,1)} collective-permute-done((bf16[1024,1024]{1,0:T(8,128)(2,1)}, bf16[1024,1024]{1,0:T(8,128)(2,1)}, u32[]{:S(2)}, u32[]{:S(2)}) %collective-permute-start.1) | collective-permute-done | bytes 2097184 | tf_op jit(solution)/shard_map/ppermute | solution.py:58
  106.7 13.9 %convolution_add_fusion = f32[2048,1792]{0,1:T(8,128)} fusion(f32[1792]{0:T(1024)S(1)} %pad_maximum_fusion.9, bf16[4096,1024]{1,0:T(8,128)(2,1)} %constant_dynamic-update-slice_fusion, s32[]{:T(128)S(6)} %select_n.70, bf16[1024,1024]{1,0:T(8,128)(2,1)S(1)} %copy-done.32, bf16[1024,256]{1,0:T(8,128)(2,1)S(1)} %copy-done.18, ...), kind=kOutput, calls=%fused_computation.77 | convolution fusion | flops 7534542848 | bytes 22551556 | tf_op jit(solution)/shard_map/dot_general | solution.py:81
  128.7 59.7 %while.31 = (s32[]{:T(128)}, bf16[4,512,4,64]{1,3,2,0:T(8,128)(2,1)}, f32[4,4,512]{2,1,0:T(4,128)}, s32[4]{0:T(128)S(1)}, bf16[2560,4,64]{0,2,1:T(8,128)(2,1)}, ...) while((s32[]{:T(128)}, ...), condition=%wide.region_6.7_spmd.clone, body=%wide.region_3.6_spmd.clone.sunk | while | flops 563084288 | bytes 29175080 | solution.py:129
  188.4 4.7 convolution_convert_fusion
  198.2 80.2 %while.32 = (s32[]{:T(128)}, f32[2048,4,64]{0,2,1:T(8,128)}, f32[2560,4,64]{0,2,1:T(8,128)}, f32[2560,4,64]{0,2,1:T(8,128)}, bf16[2560,4,64]{0,2,1:T(8,128)(2,1)...) while((s32[]{:T(128)}, f32[2048,4,64]{0,2,1:T(8,128)}, ...), condition=%wide.region_10.11_spmd.clone, body=%wide.region_8.10_spmd.clone.sunk | while | flops 1375599616 | bytes 97585616 | solution.py:199
  213.9 4.5 fusion.146
  234.0 4.5 fusion.146
  253.9 4.5 fusion.146
  285.0 26.7 %add_convert_fusion = (bf16[2048,1024]{0,1:T(8,128)(2,1)S(1)}, f32[2048,1024]{0,1:T(8,128)}) fusion(f32[2048,1792]{0,1:T(8,128)} %convolution_add_fusion, bf16[2048,1024]{1,0:T(8,128)(2,1)S(1)} %copy-done.31, bf16[1024,1024]{1,0:T(8,128)(2,1)S(1)} %copy-done), kind=kOutput, calls=%fused_computation.61 | convolution fusion | flops 4445962240 | bytes 27262976 | tf_op jit(solution)/shard_map/td,fd->tf/dot_general | solution.py:149
  313.9 12.7 %fusion.82 = f32[2048,1024]{1,0:T(8,128)} fusion(bf16[1024,1024]{1,0:T(8,128)(2,1)} %param.21, bf16[1024,256]{1,0:T(8,128)(2,1)S(1)} %copy-done.19, bf16[1024,256]{1,0:T(8,128)(2,1)S(1)} %copy-done.17, bf16[1024,256]{1,0:T(8,128)(2,1)S(1)} %copy-done.15, bf16[2048,1024]{0,1:T(8,128)(2,1)S(1)} %get-tuple-element.373, bf16[2048,256]{0,1:T(8,128)(2,1)S(1)} %bitcast.102, ...), kind=kOutput, calls=%fused_computation.123 | convolution fusion | flops 7560232960 | bytes 19398656 | tf_op jit(solution)/shard_map/tc,dc->td/dot_general | solution.py:221
  329.2 11.6 %multiply_convert_fusion.1 = bf16[2048,1024]{0,1:T(8,128)(2,1)} fusion(f32[2048,1024]{0,1:T(8,128)} %get-tuple-element.374, f32[2048,1792]{0,1:T(8,128)} %convolution_add_fusion), kind=kLoop, calls=%fused_computation.62 | loop fusion | flops 6291456 | bytes 20971520 | tf_op jit(solution)/shard_map/convert_element_type | solution.py:133
  340.8 6.6 fusion.96
  347.4 4.8 convolution_add_fusion.1
  357.0 12.4 %fusion.61 = f32[1024,1792]{1,0:T(8,128)S(1)} fusion(bf16[4096,1024]{1,0:T(8,128)(2,1)} %constant_dynamic-update-slice_fusion, s32[]{:T(128)S(6)} %select_n.70, bf16[2048,1024]{0,1:T(8,128)(2,1)} %copy-done.6, bf16[2048,256]{0,1:T(8,128)(2,1)} %bitcast.103, bf16[2048,256]{0,1:T(8,128)(2,1)} %bitcast.112, bf16[2048,256]{0,1:T(8,128)(2,1)} %bitcast.109), kind=kOutput, calls=%fused_computation.82 | convolution fusion | flops 7545552896 | bytes 18874372 | tf_op jit(solution)/shard_map/td,tc->dc/dot_general | solution.py:216
  384.6 4.7 slice.139
  389.6 10.0 %fusion.97 = f32[1024,1024]{1,0:T(8,128)} fusion(bf16[2048,1024]{0,1:T(8,128)(2,1)} %multiply_convert_fusion.1, bf16[2048,1024]{1,0:T(8,128)(2,1)} %all-gather.2.cloned.1.call-done), kind=kOutput, calls=%fused_computation.166 | convolution fusion | flops 4294967296 | bytes 12582912 | tf_op jit(solution)/shard_map/tf,td->fd/dot_general | solution.py:155
  409.2 63.7 %reduce-scatter.7.cloned.1.call-done = f32[512,1024]{1,0:T(8,128)} async-done(((f32[2048,1024]{1,0:T(8,128)}), f32[512,1024]{1,0:T(8,128)}) %reduce-scatter.7.cloned.1.call-update) | async-done | bytes 2097168 | tf_op jit(solution)/shard_map/reduce_scatter | solution.py:137
  472.9 5.1 convert_reduce_fusion.2
  478.0 40.9 %all-reduce.2 = (f32[1024]{0:T(1024)}, f32[1024]{0:T(1024)}, f32[3,16,64]{2,1,0:T(8,128)}, f32[4096]{0:T(1024)}, f32[1024]{0:T(1024)}) all-reduce(f32[1024]{0:T(1024)S(1)} %get-tuple-element.320, f32[1024]{0:T(1024)S(1)} %get-tuple-element.322, ...), channel_id=1, replica_groups=mesh['dp'=8,'tensor'=4] {'dp','tensor'}, use_global_device_ids=true, to_apply=%region_15.16 | all-reduce | flops 10240 | bytes 81920 | tf_op jit(solution)/shard_map/psum | solution.py:249
  519.0 22.8 %reduce-scatter.15.cloned.1.call-done = f32[4,64,128]{2,1,0:T(8,128)} async-done(((f32[4,64,1024]{2,1,0:T(8,128)}), f32[4,64,128]{2,1,0:T(8,128)}) %reduce-scatter.15.cloned.1.call-update) | async-done | bytes 131088 | tf_op jit(solution)/shard_map/reduce_scatter | solution.py:255
  541.8 78.1 %reduce-scatter.11.cloned.1.call-done = f32[3,128,4,64]{1,3,2,0:T(8,128)} async-done(((f32[3,1024,4,64]{1,3,2,0:T(8,128)}), f32[3,128,4,64]{1,3,2,0:T(8,128)}) %reduce-scatter.11.cloned.1.call-update) | async-done | bytes 393232 | tf_op jit(solution)/shard_map/reduce_scatter | solution.py:253
  619.8 91.5 %reduce-scatter.13.cloned.1.call-done = f32[128,1024]{1,0:T(8,128)} async-done(((f32[1024,1024]{1,0:T(8,128)}), f32[128,1024]{1,0:T(8,128)}) %reduce-scatter.13.cloned.1.call-update) | async-done | bytes 524304 | tf_op jit(solution)/shard_map/reduce_scatter | solution.py:254
  711.3 92.5 %reduce-scatter.17.cloned.1.call-done = f32[1024,128]{1,0:T(8,128)} async-done(((f32[1024,1024]{1,0:T(8,128)}), f32[1024,128]{1,0:T(8,128)}) %reduce-scatter.17.cloned.1.call-update) | async-done | bytes 524304 | tf_op jit(solution)/shard_map/reduce_scatter | solution.py:261
  (247 shorter events, 203.5 us)
Async XLA Ops:
  7.2 277.7 %copy-start = (bf16[1024,1024]{1,0:T(8,128)(2,1)S(1)}, bf16[1024,1024]{1,0:T(8,128)(2,1)}, u32[]{:S(2)}) copy-start(bf16[1024,1024]{1,0:T(8,128)(2,1)} %param.24) | copy-start | bytes 6291460
  7.2 181.2 %all-gather.2.cloned.1.call-start = ((), (), s32[]{:S(2)}) async-start(), calls=%async_computation.7 | async-start | bytes 5242880 | tf_op jit(solution)/shard_map/all_gather | solution.py:145
  11.1 35.7 %copy-start.28 = (f32[3,4,64]{2,1,0:T(4,128)S(1)}, f32[3,4,64]{2,1,0:T(4,128)}, u32[]{:S(2)}) copy-start(f32[3,4,64]{2,1,0:T(4,128)} %param.20) | copy-start | bytes 9220
  11.1 35.8 %copy-start.33 = (s32[1,4]{1,0:T(1,128)S(1)}, s32[1,4]{1,0:T(1,128)}, u32[]{:S(2)}) copy-start(s32[1,4]{1,0:T(1,128)} %param.27) | copy-start | bytes 52
  11.1 36.2 %copy-start.30 = (f32[1024]{0:T(1024)S(1)}, f32[1024]{0:T(1024)}, u32[]{:S(2)}) copy-start(f32[1024]{0:T(1024)} %param.22) | copy-start | bytes 12292
  13.8 21.5 %collective-permute-start = (bf16[512,1024]{1,0:T(8,128)(2,1)S(1)}, bf16[512,1024]{1,0:T(8,128)(2,1)}, u32[]{:S(2)}, u32[]{:S(2)}) collective-permute-start(bf16[512,1024]{1,0:T(8,128)(2,1)S(1)} %get-tuple-element.376), channel_id=1, source_target_pairs={{0,3},{1,0},{2,1},{3,2},{4,7},{5,4},{6,5},{7,6},{8,11},{9,8},{10,9... | collective-permute-start | bytes 3145736 | tf_op jit(solution)/shard_map/ppermute | solution.py:58
  16.2 387.9 %reduce-scatter.9.cloned.1.call-start = ((), (), s32[]{:S(2)}) async-start(), calls=%async_computation.8 | async-start | bytes 10485760 | tf_op jit(solution)/shard_map/reduce_scatter | solution.py:220
  38.1 59.0 %collective-permute-start.1 = (bf16[1024,1024]{1,0:T(8,128)(2,1)}, bf16[1024,1024]{1,0:T(8,128)(2,1)}, u32[]{:S(2)}, u32[]{:S(2)}) collective-permute-start(bf16[1024,1024]{1,0:T(8,128)(2,1)} %pad_maximum_fusion.3), channel_id=1, source_target_pairs={{0,2},{1,3},{2,0},{3,1},{4,6},{5,7},{6,4},{7,5},{8,10},{9,11},{10,... | collective-permute-start | bytes 6291464 | tf_op jit(solution)/shard_map/ppermute | solution.py:58
  48.3 76.8 %copy-start.11 = (f32[2048,8]{0,1:T(8,128)}, f32[2048,8]{0,1:T(8,128)S(1)}, u32[]{:S(2)}) copy-start(f32[2048,8]{0,1:T(8,128)S(1)} %get-tuple-element.406) | copy-start | bytes 196612
  48.3 58.4 %copy-start.14 = (bf16[1024,256]{1,0:T(8,128)(2,1)S(1)}, bf16[1024,256]{1,0:T(8,128)(2,1)}, u32[]{:S(2)}) copy-start(bf16[1024,256]{1,0:T(8,128)(2,1)} %copy.36) | copy-start | bytes 1572868
  48.3 58.4 %copy-start.16 = (bf16[1024,256]{1,0:T(8,128)(2,1)S(1)}, bf16[1024,256]{1,0:T(8,128)(2,1)}, u32[]{:S(2)}) copy-start(bf16[1024,256]{1,0:T(8,128)(2,1)} %copy.37) | copy-start | bytes 1572868
  48.3 58.4 %copy-start.18 = (bf16[1024,256]{1,0:T(8,128)(2,1)S(1)}, bf16[1024,256]{1,0:T(8,128)(2,1)}, u32[]{:S(2)}) copy-start(bf16[1024,256]{1,0:T(8,128)(2,1)} %copy.38) | copy-start | bytes 1572868
  48.3 58.4 %copy-start.32 = (bf16[1024,1024]{1,0:T(8,128)(2,1)S(1)}, bf16[1024,1024]{1,0:T(8,128)(2,1)}, u32[]{:S(2)}) copy-start(bf16[1024,1024]{1,0:T(8,128)(2,1)} %param.21) | copy-start | bytes 6291460
  198.2 83.4 %copy-start.12 = (f32[2048,8]{0,1:T(8,128)S(1)}, f32[2048,8]{0,1:T(8,128)}, u32[]{:S(2)}) copy-start(f32[2048,8]{0,1:T(8,128)} %copy-done.11) | copy-start | bytes 196612
  198.2 83.5 %copy-start.20 = (f32[2048,8]{0,1:T(8,128)S(1)}, f32[2048,8]{0,1:T(8,128)}, u32[]{:S(2)}) copy-start(f32[2048,8]{0,1:T(8,128)} %get-tuple-element.404) | copy-start | bytes 196612
  285.0 28.9 %copy-start.15 = (bf16[1024,256]{1,0:T(8,128)(2,1)S(1)}, bf16[1024,256]{1,0:T(8,128)(2,1)}, u32[]{:S(2)}) copy-start(bf16[1024,256]{1,0:T(8,128)(2,1)} %copy.36) | copy-start | bytes 1572868
  285.0 28.9 %copy-start.17 = (bf16[1024,256]{1,0:T(8,128)(2,1)S(1)}, bf16[1024,256]{1,0:T(8,128)(2,1)}, u32[]{:S(2)}) copy-start(bf16[1024,256]{1,0:T(8,128)(2,1)} %copy.37) | copy-start | bytes 1572868
  285.0 28.9 %copy-start.19 = (bf16[1024,256]{1,0:T(8,128)(2,1)S(1)}, bf16[1024,256]{1,0:T(8,128)(2,1)}, u32[]{:S(2)}) copy-start(bf16[1024,256]{1,0:T(8,128)(2,1)} %copy.38) | copy-start | bytes 1572868
  326.6 146.3 %reduce-scatter.7.cloned.1.call-start = ((), (), s32[]{:S(2)}) async-start(), calls=%async_computation.6 | async-start | bytes 10485760 | tf_op jit(solution)/shard_map/reduce_scatter | solution.py:137
  352.2 189.5 %reduce-scatter.15.cloned.1.call-start = ((), (), s32[]{:S(2)}) async-start(), calls=%async_computation.11 | async-start | bytes 1179648 | tf_op jit(solution)/shard_map/reduce_scatter | solution.py:255
  356.7 263.1 %reduce-scatter.11.cloned.1.call-start = ((), (), s32[]{:S(2)}) async-start(), calls=%async_computation.9 | async-start | bytes 3538944 | tf_op jit(solution)/shard_map/reduce_scatter | solution.py:253
  384.5 326.8 %reduce-scatter.13.cloned.1.call-start = ((), (), s32[]{:S(2)}) async-start(), calls=%async_computation.10 | async-start | bytes 4718592 | tf_op jit(solution)/shard_map/reduce_scatter | solution.py:254
  389.3 414.6 %reduce-scatter.17.cloned.1.call-start = ((), (), s32[]{:S(2)}) async-start(), calls=%async_computation.12 | async-start | bytes 4718592 | tf_op jit(solution)/shard_map/reduce_scatter | solution.py:261
  399.7 73.2 %copy-start.29 = (f32[1024]{0:T(1024)S(1)}, f32[1024]{0:T(1024)}, u32[]{:S(2)}) copy-start(f32[1024]{0:T(1024)} %param.25) | copy-start | bytes 12292
  (32 other events, 190.6 us)
Sparse Core Ops, SparseCore 0:
  16.4 47.4 all-gather.1
  326.7 72.0 reduce-scatter.8
  401.4 71.4 reduce-scatter.6
  476.7 64.9 reduce-scatter.14
  545.8 74.0 reduce-scatter.10
  623.9 87.3 reduce-scatter.12
  715.5 88.3 reduce-scatter.16
